TPU v7x, 32 devices: a whole 2x2x4 slice. The times are simulated.
32 devices in a mesh: row: 4 (over y, x), col: 8 (over z, core).
Axes of the slice: x: 2, y: 2, z: 4, core: 2. Of those that a mesh axis runs over, the one named last changes fastest.
Arguments:
- loads: float32 [4, 8, 1024, 8], P('row', 'col'), may hold values from -6 to 6
- schur: float32 [4, 8, 1024, 1024], P('row', 'col'), may hold values from -0.5 to 4.5, as said below
- factor: float32 [4, 8, 1024, 1024], P('row', 'col'), may hold values from -0.5 to 0.6, as said below
- coarse_inverse: float32 [1536, 1536], P(('row', 'col')), may hold values from -0.5 to 1.5, as said below
- elements: int32 [4, 8], P('row', 'col'), may hold values from 4096 to 16383
- west_map: int32 [4, 8, 256], P('row', 'col'), may hold values from 0 to 255, each once within a row
- south_map: int32 [4, 8, 256], P('row', 'col'), may hold values from 0 to 255, each once within a row
- prim_local: int32 [4, 8, 48], P('row', 'col'), may hold values from 0 to 1023
- prim_coarse: int32 [4, 8, 48], P('row', 'col'), may hold values from 0 to 1535
Outputs:
- solution: float32 [4, 8, 1024, 8], P('row', 'col')
- residual: float32 [4, 8, 1024, 8], P('row', 'col')
Inputs may be any that keep to these rules, and one draw needn't show every extreme that they name: `schur`: symmetric positive definite. `factor`: symmetric positive definite. `coarse_inverse`: symmetric positive definite. `west_map`: each subdomain's row is a permutation of 0 to 255. `south_map`: each subdomain's row is a permutation of 0 to 255. `prim_local`: values may repeat. `prim_coarse`: values may repeat, within a subdomain and between subdomains.
All inputs are finite; a program needn't handle non-finite values.
Results may differ from a plain program's by a relative error of at most 0.0001.
Values sent between devices are 32-bit elements; how exact they have to be, the bound alone decides.
A program may use at most 128 MiB of HBM per device.

v0:
```python
import jax
import jax.numpy as jnp
from jax import lax
from jax.sharding import PartitionSpec as P

ELEM_BASE = 4096
HIGHEST_PRECISION = lax.Precision.HIGHEST


def from_behind(x, axis, by):
    devices = lax.axis_size(axis)
    pairs = [(i, i + by) for i in range(devices) if 0 <= i + by < devices]
    return lax.ppermute(x, axis, pairs)


def product(matrix, vectors):
    return jnp.dot(matrix, vectors, precision=HIGHEST_PRECISION, preferred_element_type=jnp.float32)


def body(
    loads, schur, factor, coarse_inverse, elements, west_map, south_map, prim_local, prim_coarse
):
    schur_block = schur[0, 0]
    factor_block = factor[0, 0]
    local_loads = loads[0, 0]
    sweep_count = elements[0, 0] // ELEM_BASE
    west_order = west_map[0, 0]
    south_order = south_map[0, 0]
    primal_local = prim_local[0, 0]
    primal_coarse = prim_coarse[0, 0]
    unknowns = schur_block.shape[0]
    face_size = unknowns // 4
    column = lax.axis_index("col")
    grid_row = lax.axis_index("row")
    neighbour_flags = jnp.stack(
        [
            column > 0,
            column < lax.axis_size("col") - 1,
            grid_row > 0,
            grid_row < lax.axis_size("row") - 1,
        ]
    )
    weights = jnp.where(neighbour_flags[jnp.arange(unknowns) // face_size], 0.5, 1.0).astype(
        jnp.float32
    )[:, None]

    def assemble(values):
        west_face = values[:face_size]
        east_face = values[face_size : 2 * face_size]
        south_face = values[2 * face_size : 3 * face_size]
        north_face = values[3 * face_size :]
        from_west = from_behind(east_face, "col", 1)
        west_add = jnp.take(from_west, west_order, axis=0)
        west_back = jnp.zeros_like(west_face).at[west_order].set(west_face)
        from_east = from_behind(west_back, "col", -1)
        from_south = from_behind(north_face, "row", 1)
        south_add = jnp.take(from_south, south_order, axis=0)
        south_back = jnp.zeros_like(south_face).at[south_order].set(south_face)
        from_north = from_behind(south_back, "row", -1)
        return values + jnp.concatenate([west_add, from_east, south_add, from_north], axis=0)

    def weighted_sum(first, second):
        return jnp.sum(weights * first * second, axis=0)

    all_primal = lax.all_gather(primal_coarse, ("row", "col"), axis=0, tiled=True)
    right_side = assemble(local_loads)
    residual = right_side
    scaled = weights * residual
    local = product(factor_block, scaled)

    def sweep(turn, present):
        return present + product(factor_block, scaled - product(schur_block, present))

    local = lax.fori_loop(1, sweep_count, sweep, local)
    picked = jnp.take(scaled, primal_local, axis=0)
    columns = jnp.take(coarse_inverse, all_primal, axis=1)
    solved = product(columns, lax.all_gather(picked, ("row", "col"), axis=0, tiled=True))
    whole = lax.all_gather(solved, ("row", "col"), axis=0, tiled=True)
    precond = assemble(
        weights
        * (
            local
            + jnp.zeros_like(scaled).at[primal_local].add(jnp.take(whole, primal_coarse, axis=0))
        )
    )
    product_now = lax.psum(weighted_sum(residual, precond), ("row", "col"))
    image = assemble(product(schur_block, precond))
    alpha = product_now / lax.psum(weighted_sum(precond, image), ("row", "col"))
    solution = alpha * precond
    residual = residual - alpha * image
    return (solution[None, None], residual[None, None])


def solution(mesh):
    placed = (
        P("row", "col", None, None),
        P("row", "col", None, None),
        P("row", "col", None, None),
        P(("row", "col"), None),
        P("row", "col"),
        P("row", "col", None),
        P("row", "col", None),
        P("row", "col", None),
        P("row", "col", None),
    )
    return jax.shard_map(
        body,
        mesh=mesh,
        in_specs=placed,
        out_specs=(P("row", "col", None, None), P("row", "col", None, None)),
        check_vma=False,
    )
```

profile of v0, /device:TPU:0, one launch (start us, length us, event | category | flops | bytes accessed | tf_op | source)
XLA Modules:
  0.0 256.3 jit_solution(8718719181798448319)
XLA Ops:
  0.6 0.7 compare_select_fusion.3
  1.3 0.7 fusion.39
  2.2 1.2 scatter_custom_fusion
  3.5 1.3 collective-permute-start.1
  4.8 0.7 compare_select_fusion.2
  5.6 1.2 scatter_custom_fusion.1
  6.8 1.3 collective-permute-start.3
  8.3 5.5 %collective-permute-start.2 = (f32[256,8]{1,0:T(8,128)S(1)}, f32[256,8]{1,0:T(8,128)S(1)}, u32[]{:S(2)}, u32[]{:S(2)}) collective-permute-start(f32[256,8]{1,0:T(8,128)S(1)} %bitcast.105), channel_id=1, source_target_pairs={{0,8},{8,16},{16,24},{1,9},{9,17},{17,25},{2,10},{10,18},{18,26},{... | collective-permute-start | bytes 24584 | tf_op jit(solution)/shard_map/ppermute | solution.py:13
  13.9 2.8 %collective-permute-start = (f32[256,8]{1,0:T(8,128)S(1)}, f32[256,8]{1,0:T(8,128)S(1)}, u32[]{:S(2)}, u32[]{:S(2)}) collective-permute-start(f32[256,8]{1,0:T(8,128)S(1)} %bitcast.104), channel_id=1, source_target_pairs={{0,1},{1,2},{2,3},{3,4},{4,5},{5,6},{6,7},{8,9},{9,10},{10,11},{11... | collective-permute-start | bytes 24584 | tf_op jit(solution)/shard_map/ppermute | solution.py:13
  19.3 0.7 compare_and_fusion.2
  20.0 0.7 compare_select_fusion.5
  20.7 0.7 compare_and_fusion.1
  21.4 0.7 compare_select_fusion.4
  22.1 0.7 bitcast_dynamic-update-slice_fusion
  22.8 41.8 %all-reduce = s32[1536]{0:T(1024)S(1)} all-reduce(s32[1536]{0:T(1024)S(1)} %bitcast_dynamic-update-slice_fusion), channel_id=2, replica_groups=mesh['row'=4,'col'=8] {'row','col'}, use_global_device_ids=true, to_apply=%add | all-reduce | flops 1536 | bytes 12288 | tf_op jit(solution)/shard_map/all_gather | solution.py:65
  65.4 1.2 copy.96
  66.6 2.6 %gather_fusion = f32[1536,48]{1,0:T(8,128)S(1)} fusion(f32[48,1536]{0,1:T(8,128)S(1)} %copy.96, s32[2048]{0:T(1024)S(1)} %pad_clamp_fusion), kind=kCustom, calls=%fused_computation.6 | custom fusion | bytes 595968 | tf_op jit(solution)/shard_map/jit(_take)/gather | solution.py:76
  69.2 0.7 gather_fusion.3
  70.0 0.7 gather_fusion.2
  71.1 5.7 %convolution_bitcast_fusion.2 = f32[1024,8]{0,1:T(8,128)S(1)} fusion(f32[1,1,1024,8]{2,3,1,0:T(8,128)S(1)} %copy-done.1, f32[1,1,256,8]{2,3,1,0:T(8,128)S(1)} %bitcast.107, f32[1,1,256,8]{2,3,1,0:T(8,128)S(1)} %bitcast.102, f32[1,1,256,8]{2,3,1,0:T(8,128)S(1)} %bitcast.106, f32[1,1,256,8]{2,3,1,0:T(8,128)S(1)} %bitcast.103, f32[1024]{0:T(1024)S(1)} %bitcast.98, ...), kind=kOutput, calls=%fused_computation.20 | convolution fusion | flops 100704256 | bytes 4296704 | tf_op jit(solution)/shard_map/dot_general | solution.py:17
  76.8 19.1 %while.10 = (s32[]{:T(128)}, f32[1024,8]{0,1:T(8,128)S(1)}, s32[]{:T(128)}, f32[1024,1024]{1,0:T(8,128)}, f32[1024,8]{0,1:T(8,128)S(1)}, /*index=5*/f32[1024,1024]{1,0:T(8,128)}, s32[]{:T(128)}) while((s32[]{:T(128)}, f32[1024,8]{0,1:T(8,128)S(1)}, s32[]{:T(128)}, f32[1024,1024]{1,0:T(8,128)}, f32[1024,8]{0,1:T(8,128)S(1)}, ...), condition=%wide.region_3.5_spmd, body=%wide.region_2.4_spmd.sunk | while | flops 201342976 | bytes 25362536 | solution.py:74
  76.9 5.9 %convolution_subtract_fusion.2 = f32[1024,8]{0,1:T(8,128)S(1)} fusion(f32[1024,8]{0,1:T(8,128)S(1)} %get-tuple-element.125, f32[1024,1024]{1,0:T(8,128)} %get-tuple-element.124, f32[1024,8]{0,1:T(8,128)S(1)} %get-tuple-element.115), kind=kOutput, calls=%fused_computation.18.clone.1 | convolution fusion | flops 100671488 | bytes 4292608 | tf_op jit(solution)/shard_map/while/body/dot_general | solution.py:17
  82.8 3.6 %fusion.55 = f32[1024,8]{0,1:T(8,128)S(1)} fusion(f32[1024,8]{0,1:T(8,128)S(1)} %get-tuple-element.115, f32[1024,8]{0,1:T(8,128)S(1)} %convolution_subtract_fusion.2, f32[1024,1024]{1,0:T(8,128)S(1)} %copy-done), kind=kOutput, calls=%fused_computation.17.clone.1 | convolution fusion | flops 100671488 | bytes 4292608 | tf_op jit(solution)/shard_map/while/body/dot_general | solution.py:17
  86.4 5.9 %convolution_subtract_fusion.2 = f32[1024,8]{0,1:T(8,128)S(1)} fusion(f32[1024,8]{0,1:T(8,128)S(1)} %get-tuple-element.125, f32[1024,1024]{1,0:T(8,128)} %get-tuple-element.124, f32[1024,8]{0,1:T(8,128)S(1)} %get-tuple-element.115), kind=kOutput, calls=%fused_computation.18.clone.1 | convolution fusion | flops 100671488 | bytes 4292608 | tf_op jit(solution)/shard_map/while/body/dot_general | solution.py:17
  92.3 3.6 %fusion.55 = f32[1024,8]{0,1:T(8,128)S(1)} fusion(f32[1024,8]{0,1:T(8,128)S(1)} %get-tuple-element.115, f32[1024,8]{0,1:T(8,128)S(1)} %convolution_subtract_fusion.2, f32[1024,1024]{1,0:T(8,128)S(1)} %copy-done), kind=kOutput, calls=%fused_computation.17.clone.1 | convolution fusion | flops 100671488 | bytes 4292608 | tf_op jit(solution)/shard_map/while/body/dot_general | solution.py:17
  96.8 37.1 %all-gather.1 = f32[32,48,8]{1,2,0:T(8,128)S(1)} all-gather(f32[1,48,8]{1,2,0:T(8,128)S(1)} %copy.98), channel_id=1, replica_groups=mesh['row'=4,'col'=8] {'row','col'}, dimensions={0}, use_global_device_ids=true | all-gather | bytes 50688 | tf_op jit(solution)/shard_map/all_gather | solution.py:77
  134.7 38.6 %all-gather.2 = f32[32,48,8]{1,2,0:T(8,128)S(1)} all-gather(f32[1,48,8]{1,2,0:T(8,128)S(1)} %convolution_bitcast_fusion.3), channel_id=1, replica_groups=mesh['row'=4,'col'=8] {'row','col'}, dimensions={0}, use_global_device_ids=true | all-gather | bytes 50688 | tf_op jit(solution)/shard_map/all_gather | solution.py:78
  173.5 1.1 scatter_custom_fusion.2
  174.9 1.3 collective-permute-start.6
  176.1 2.2 collective-permute-start.4
  178.5 1.2 scatter_custom_fusion.4
  179.8 1.3 collective-permute-start.7
  181.2 1.2 scatter_custom_fusion.3
  182.5 1.5 collective-permute-start.5
  184.1 0.7 gather_fusion.5
  185.1 0.7 gather_fusion.4
  185.9 3.0 %collective-permute-done.7 = f32[256,8]{0,1:T(8,128)S(1)} collective-permute-done((f32[256,8]{0,1:T(8,128)S(1)}, f32[256,8]{0,1:T(8,128)S(1)}, u32[]{:S(2)}, u32[]{:S(2)}) %collective-permute-start.7) | collective-permute-done | bytes 8224 | tf_op jit(solution)/shard_map/ppermute | solution.py:13
  188.9 5.6 %convolution_bitcast_fusion.1 = f32[1024,8]{0,1:T(8,128)S(1)} fusion(f32[1024,8]{0,1:T(8,128)S(1)} %maximum_add_fusion.2, f32[1,1,1024,1024]{3,2,1,0:T(8,128)} %bitcast.95), kind=kOutput, calls=%fused_computation.19 | convolution fusion | flops 100663296 | bytes 4259840 | tf_op jit(solution)/shard_map/dot_general | solution.py:17
  194.6 5.9 %collective-permute-start.10 = (f32[256,8]{0,1:T(8,128)S(1)}, f32[256,8]{0,1:T(8,128)S(1)}, u32[]{:S(2)}, u32[]{:S(2)}) collective-permute-start(f32[256,8]{0,1:T(8,128)S(1)} %get-tuple-element.55), channel_id=1, source_target_pairs={{0,8},{8,16},{16,24},{1,9},{9,17},{17,25},{2,10},{10,18},{18,26},{... | collective-permute-start | bytes 24584 | tf_op jit(solution)/shard_map/ppermute | solution.py:13
  200.6 4.0 %collective-permute-start.8 = (f32[256,8]{0,1:T(8,128)S(1)}, f32[256,8]{0,1:T(8,128)S(1)}, u32[]{:S(2)}, u32[]{:S(2)}) collective-permute-start(f32[256,8]{0,1:T(8,128)S(1)} %get-tuple-element.53), channel_id=1, source_target_pairs={{0,1},{1,2},{2,3},{3,4},{4,5},{5,6},{6,7},{8,9},{9,10},{10,11},{11... | collective-permute-start | bytes 24584 | tf_op jit(solution)/shard_map/ppermute | solution.py:13
  204.7 1.2 scatter_custom_fusion.6
  206.0 1.3 collective-permute-start.11
  207.4 1.2 scatter_custom_fusion.5
  208.7 1.3 collective-permute-start.9
  210.1 0.7 gather_fusion.7
  211.0 0.7 gather_fusion.6
  212.5 43.1 %all-reduce.1 = (f32[8]{0:T(128)S(1)}, f32[8]{0:T(128)S(1)}) all-reduce(f32[8]{0:T(128)S(1)} %get-tuple-element.38, f32[8]{0:T(128)S(1)} %get-tuple-element.37), channel_id=1, replica_groups=mesh['row'=4,'col'=8] {'row','col'}, use_global_device_ids=true, to_apply=%region_8.10 | all-reduce | flops 16 | bytes 128 | tf_op jit(solution)/shard_map/psum | solution.py:86
  255.6 0.7 subtract_bitcast_fusion
  (76 shorter events, 8.0 us)
Async XLA Ops:
  0.6 70.3 %copy-start.1 = (f32[1,1,1024,8]{2,3,1,0:T(8,128)S(1)}, f32[1,1,1024,8]{2,3,1,0:T(8,128)}, u32[]{:S(2)}) copy-start(f32[1,1,1024,8]{2,3,1,0:T(8,128)} %param.13) | copy-start | bytes 98308
  3.5 67.4 %collective-permute-start.1 = (f32[256,8]{0,1:T(8,128)S(1)}, f32[256,8]{0,1:T(8,128)S(1)}, u32[]{:S(2)}, u32[]{:S(2)}) collective-permute-start(f32[256,8]{0,1:T(8,128)S(1)} %copy.91), channel_id=1, source_target_pairs={{1,0},{2,1},{3,2},{4,3},{5,4},{6,5},{7,6},{9,8},{10,9},{11,10},{12... | collective-permute-start | bytes 24584 | tf_op jit(solution)/shard_map/ppermute | solution.py:13
  6.8 64.0 %collective-permute-start.3 = (f32[256,8]{0,1:T(8,128)S(1)}, f32[256,8]{0,1:T(8,128)S(1)}, u32[]{:S(2)}, u32[]{:S(2)}) collective-permute-start(f32[256,8]{0,1:T(8,128)S(1)} %copy.95), channel_id=1, source_target_pairs={{8,0},{16,8},{24,16},{9,1},{17,9},{25,17},{10,2},{18,10},{26,18},{... | collective-permute-start | bytes 24584 | tf_op jit(solution)/shard_map/ppermute | solution.py:13
  8.3 61.0 %collective-permute-start.2 = (f32[256,8]{1,0:T(8,128)S(1)}, f32[256,8]{1,0:T(8,128)S(1)}, u32[]{:S(2)}, u32[]{:S(2)}) collective-permute-start(f32[256,8]{1,0:T(8,128)S(1)} %bitcast.105), channel_id=1, source_target_pairs={{0,8},{8,16},{16,24},{1,9},{9,17},{17,25},{2,10},{10,18},{18,26},{... | collective-permute-start | bytes 24584 | tf_op jit(solution)/shard_map/ppermute | solution.py:13
  13.9 56.1 %collective-permute-start = (f32[256,8]{1,0:T(8,128)S(1)}, f32[256,8]{1,0:T(8,128)S(1)}, u32[]{:S(2)}, u32[]{:S(2)}) collective-permute-start(f32[256,8]{1,0:T(8,128)S(1)} %bitcast.104), channel_id=1, source_target_pairs={{0,1},{1,2},{2,3},{3,4},{4,5},{5,6},{6,7},{8,9},{9,10},{10,11},{11... | collective-permute-start | bytes 24584 | tf_op jit(solution)/shard_map/ppermute | solution.py:13
  76.9 5.9 %copy-start = (f32[1024,1024]{1,0:T(8,128)S(1)}, f32[1024,1024]{1,0:T(8,128)}, u32[]{:S(2)}) copy-start(f32[1024,1024]{1,0:T(8,128)} %get-tuple-element.126) | copy-start | bytes 12582916 | tf_op jit(solution)/shard_map/while
  86.4 5.9 %copy-start = (f32[1024,1024]{1,0:T(8,128)S(1)}, f32[1024,1024]{1,0:T(8,128)}, u32[]{:S(2)}) copy-start(f32[1024,1024]{1,0:T(8,128)} %get-tuple-element.126) | copy-start | bytes 12582916 | tf_op jit(solution)/shard_map/while
  174.9 9.1 %collective-permute-start.6 = (f32[256,8]{0,1:T(8,128)S(1)}, f32[256,8]{0,1:T(8,128)S(1)}, u32[]{:S(2)}, u32[]{:S(2)}) collective-permute-start(f32[256,8]{0,1:T(8,128)S(1)} %get-tuple-element.59), channel_id=1, source_target_pairs={{0,8},{8,16},{16,24},{1,9},{9,17},{17,25},{2,10},{10,18},{18,26},{... | collective-permute-start | bytes 24584 | tf_op jit(solution)/shard_map/ppermute | solution.py:13
  176.1 8.8 %collective-permute-start.4 = (f32[256,8]{0,1:T(8,128)S(1)}, f32[256,8]{0,1:T(8,128)S(1)}, u32[]{:S(2)}, u32[]{:S(2)}) collective-permute-start(f32[256,8]{0,1:T(8,128)S(1)} %get-tuple-element.57), channel_id=1, source_target_pairs={{0,1},{1,2},{2,3},{3,4},{4,5},{5,6},{6,7},{8,9},{9,10},{10,11},{11... | collective-permute-start | bytes 24584 | tf_op jit(solution)/shard_map/ppermute | solution.py:13
  179.8 9.1 %collective-permute-start.7 = (f32[256,8]{0,1:T(8,128)S(1)}, f32[256,8]{0,1:T(8,128)S(1)}, u32[]{:S(2)}, u32[]{:S(2)}) collective-permute-start(f32[256,8]{0,1:T(8,128)S(1)} %copy.111), channel_id=1, source_target_pairs={{8,0},{16,8},{24,16},{9,1},{17,9},{25,17},{10,2},{18,10},{26,18},{... | collective-permute-start | bytes 24584 | tf_op jit(solution)/shard_map/ppermute | solution.py:13
  182.5 6.4 %collective-permute-start.5 = (f32[256,8]{0,1:T(8,128)S(1)}, f32[256,8]{0,1:T(8,128)S(1)}, u32[]{:S(2)}, u32[]{:S(2)}) collective-permute-start(f32[256,8]{0,1:T(8,128)S(1)} %copy.107), channel_id=1, source_target_pairs={{1,0},{2,1},{3,2},{4,3},{5,4},{6,5},{7,6},{9,8},{10,9},{11,10},{12... | collective-permute-start | bytes 24584 | tf_op jit(solution)/shard_map/ppermute | solution.py:13
  194.6 15.4 %collective-permute-start.10 = (f32[256,8]{0,1:T(8,128)S(1)}, f32[256,8]{0,1:T(8,128)S(1)}, u32[]{:S(2)}, u32[]{:S(2)}) collective-permute-start(f32[256,8]{0,1:T(8,128)S(1)} %get-tuple-element.55), channel_id=1, source_target_pairs={{0,8},{8,16},{16,24},{1,9},{9,17},{17,25},{2,10},{10,18},{18,26},{... | collective-permute-start | bytes 24584 | tf_op jit(solution)/shard_map/ppermute | solution.py:13
  200.6 10.4 %collective-permute-start.8 = (f32[256,8]{0,1:T(8,128)S(1)}, f32[256,8]{0,1:T(8,128)S(1)}, u32[]{:S(2)}, u32[]{:S(2)}) collective-permute-start(f32[256,8]{0,1:T(8,128)S(1)} %get-tuple-element.53), channel_id=1, source_target_pairs={{0,1},{1,2},{2,3},{3,4},{4,5},{5,6},{6,7},{8,9},{9,10},{10,11},{11... | collective-permute-start | bytes 24584 | tf_op jit(solution)/shard_map/ppermute | solution.py:13
  206.0 6.2 %collective-permute-start.11 = (f32[256,8]{0,1:T(8,128)S(1)}, f32[256,8]{0,1:T(8,128)S(1)}, u32[]{:S(2)}, u32[]{:S(2)}) collective-permute-start(f32[256,8]{0,1:T(8,128)S(1)} %copy.119), channel_id=1, source_target_pairs={{8,0},{16,8},{24,16},{9,1},{17,9},{25,17},{10,2},{18,10},{26,18},{... | collective-permute-start | bytes 24584 | tf_op jit(solution)/shard_map/ppermute | solution.py:13
  208.7 3.7 %collective-permute-start.9 = (f32[256,8]{0,1:T(8,128)S(1)}, f32[256,8]{0,1:T(8,128)S(1)}, u32[]{:S(2)}, u32[]{:S(2)}) collective-permute-start(f32[256,8]{0,1:T(8,128)S(1)} %copy.115), channel_id=1, source_target_pairs={{1,0},{2,1},{3,2},{4,3},{5,4},{6,5},{7,6},{9,8},{10,9},{11,10},{12... | collective-permute-start | bytes 24584 | tf_op jit(solution)/shard_map/ppermute | solution.py:13
where the time goes:
time: 257 us; the launch traced here: 256 us
  blocking collectives  161 us (63%)
  matrix products  30.9 us (12%)
  starting transfers between devices  29.8 us (12%)
  local copies, waits for them, and re-layouts  20.7 us (8%)
  other arithmetic  8.95 us (3%)
  waiting for transfers between devices  3.55 us (1%)
    psum x1, blocking collectives, body(): product_now = lax.psum(weighted_sum(residual, precond), ('row', 'col'))  43.1 us
    all_gather x1, blocking collectives, body(): lax.all_gather(primal_coarse, ('row', 'col'), axis=0, tiled=True)  41.8 us
    all_gather x1, blocking collectives, body(): whole = lax.all_gather(solved, ('row', 'col'), axis=0, tiled=True)  38.6 us
    all_gather x1, blocking collectives, body(): lax.all_gather(picked, ('row', 'col'), axis=0, tiled=True)  37.1 us
    dot_general x7, matrix products, product(): jnp.dot(matrix, vectors, precision=HIGHEST_PRECISION, preferred_element_t...  30.9 us
    ppermute x12, starting transfers between devices, from_behind(): return lax.ppermute(x, axis, pairs)  29.8 us
  transfers between devices with their start and end apart: 12, of which 3 were waited for; matrix products, arithmetic and copies ran while one was open for 9% of the time, Pallas kernels for 0%

commit v1 on v0

--- a/solution.py
+++ b/solution.py
@@ -5,6 +5,11 @@
 
 ELEM_BASE = 4096
 HIGHEST_PRECISION = lax.Precision.HIGHEST
+
+
+def one_after_other(array, leading, second_2):
+    partial = lax.psum(array, leading)
+    return lax.psum(partial, second_2)
 
 
 def from_behind(x, axis, by):
@@ -83,7 +88,7 @@
             + jnp.zeros_like(scaled).at[primal_local].add(jnp.take(whole, primal_coarse, axis=0))
         )
     )
-    product_now = lax.psum(weighted_sum(residual, precond), ("row", "col"))
+    product_now = one_after_other(weighted_sum(residual, precond), "row", "col")
     image = assemble(product(schur_block, precond))
     alpha = product_now / lax.psum(weighted_sum(precond, image), ("row", "col"))
     solution = alpha * precond

time: 257 us -> 280 us (1.089)
  blocking collectives: 161 us -> 184 us
    psum x1 -> x3, blocking collectives: 43.1 us -> 66.2 us  [the longest x1 41.7 us: body(): alpha = product_now / lax.psum(weighted_sum(precond, image), ('row', 'col'))]
  transfers between devices with their start and end apart: 12 -> 12, of which waited for: 3 -> 3; matrix products, arithmetic and copies ran while one was open for 9% -> 8% of each run, Pallas kernels for 0% -> 0%
where the time goes in v1:
time: 280 us; the launch traced here: 279 us
  blocking collectives  184 us (66%)
  matrix products  30.9 us (11%)
  starting transfers between devices  29.8 us (11%)
  local copies, waits for them, and re-layouts  20.7 us (7%)
  other arithmetic  8.95 us (3%)
  waiting for transfers between devices  3.55 us (1%)
    all_gather x1, blocking collectives, body(): lax.all_gather(primal_coarse, ('row', 'col'), axis=0, tiled=True)  41.8 us
    psum x1, blocking collectives, body(): alpha = product_now / lax.psum(weighted_sum(precond, image), ('row', 'col'))  41.7 us
    all_gather x1, blocking collectives, body(): whole = lax.all_gather(solved, ('row', 'col'), axis=0, tiled=True)  38.6 us
    all_gather x1, blocking collectives, body(): lax.all_gather(picked, ('row', 'col'), axis=0, tiled=True)  37.1 us
    dot_general x7, matrix products, product(): jnp.dot(matrix, vectors, precision=HIGHEST_PRECISION, preferred_element_t...  30.9 us
    ppermute x12, starting transfers between devices, from_behind(): return lax.ppermute(x, axis, pairs)  29.8 us
    psum x1, blocking collectives, one_after_other(): return lax.psum(partial, second_2)  13.7 us
    psum x1, blocking collectives, one_after_other(): partial = lax.psum(array, leading)  10.7 us
  transfers between devices with their start and end apart: 12, of which 3 were waited for; matrix products, arithmetic and copies ran while one was open for 8% of the time, Pallas kernels for 0%

profile of v1, /device:TPU:0, one launch (start us, length us, event | category | flops | bytes accessed | tf_op | source)
XLA Modules:
  0.0 279.4 jit_solution(9304066787464615929)
XLA Ops:
  0.6 0.7 compare_select_fusion.3
  1.3 0.7 fusion.39
  2.2 1.2 scatter_custom_fusion
  3.5 1.3 collective-permute-start.1
  4.8 0.7 compare_select_fusion.2
  5.6 1.2 scatter_custom_fusion.1
  6.8 1.3 collective-permute-start.3
  8.3 5.5 %collective-permute-start.2 = (f32[256,8]{1,0:T(8,128)S(1)}, f32[256,8]{1,0:T(8,128)S(1)}, u32[]{:S(2)}, u32[]{:S(2)}) collective-permute-start(f32[256,8]{1,0:T(8,128)S(1)} %bitcast.105), channel_id=1, source_target_pairs={{0,8},{8,16},{16,24},{1,9},{9,17},{17,25},{2,10},{10,18},{18,26},{... | collective-permute-start | bytes 24584 | tf_op jit(solution)/shard_map/ppermute | solution.py:18
  13.9 2.8 collective-permute-start
  19.3 0.7 compare_and_fusion.2
  20.7 0.7 compare_and_fusion.1
  22.1 0.7 bitcast_dynamic-update-slice_fusion
  22.8 41.8 %all-reduce = s32[1536]{0:T(1024)S(1)} all-reduce(s32[1536]{0:T(1024)S(1)} %bitcast_dynamic-update-slice_fusion), channel_id=2, replica_groups=mesh['row'=4,'col'=8] {'row','col'}, use_global_device_ids=true, to_apply=%add | all-reduce | flops 1536 | bytes 12288 | tf_op jit(solution)/shard_map/all_gather | solution.py:70
  65.4 1.2 copy.96
  66.6 2.6 gather_fusion
  69.2 0.7 gather_fusion.3
  70.0 0.7 gather_fusion.2
  71.1 5.7 %convolution_bitcast_fusion.2 = f32[1024,8]{0,1:T(8,128)S(1)} fusion(f32[1,1,1024,8]{2,3,1,0:T(8,128)S(1)} %copy-done.1, f32[1,1,256,8]{2,3,1,0:T(8,128)S(1)} %bitcast.107, f32[1,1,256,8]{2,3,1,0:T(8,128)S(1)} %bitcast.102, f32[1,1,256,8]{2,3,1,0:T(8,128)S(1)} %bitcast.106, f32[1,1,256,8]{2,3,1,0:T(8,128)S(1)} %bitcast.103, f32[1024]{0:T(1024)S(1)} %bitcast.98, ...), kind=kOutput, calls=%fused_computation.20 | convolution fusion | flops 100704256 | bytes 4296704 | tf_op jit(solution)/shard_map/dot_general | solution.py:22
  76.8 19.1 %while.10 = (s32[]{:T(128)}, f32[1024,8]{0,1:T(8,128)S(1)}, s32[]{:T(128)}, f32[1024,1024]{1,0:T(8,128)}, f32[1024,8]{0,1:T(8,128)S(1)}, /*index=5*/f32[1024,1024]{1,0:T(8,128)}, s32[]{:T(128)}) while((s32[]{:T(128)}, f32[1024,8]{0,1:T(8,128)S(1)}, s32[]{:T(128)}, f32[1024,1024]{1,0:T(8,128)}, f32[1024,8]{0,1:T(8,128)S(1)}, ...), condition=%wide.region_3.5_spmd, body=%wide.region_2.4_spmd.sunk | while | flops 201342976 | bytes 25362536 | solution.py:79
  76.9 5.9 %convolution_subtract_fusion.2 = f32[1024,8]{0,1:T(8,128)S(1)} fusion(f32[1024,8]{0,1:T(8,128)S(1)} %get-tuple-element.123, f32[1024,1024]{1,0:T(8,128)} %get-tuple-element.122, f32[1024,8]{0,1:T(8,128)S(1)} %get-tuple-element.113), kind=kOutput, calls=%fused_computation.18.clone.1 | convolution fusion | flops 100671488 | bytes 4292608 | tf_op jit(solution)/shard_map/while/body/dot_general | solution.py:22
  82.8 3.6 %fusion.55 = f32[1024,8]{0,1:T(8,128)S(1)} fusion(f32[1024,8]{0,1:T(8,128)S(1)} %get-tuple-element.113, f32[1024,8]{0,1:T(8,128)S(1)} %convolution_subtract_fusion.2, f32[1024,1024]{1,0:T(8,128)S(1)} %copy-done), kind=kOutput, calls=%fused_computation.17.clone.1 | convolution fusion | flops 100671488 | bytes 4292608 | tf_op jit(solution)/shard_map/while/body/dot_general | solution.py:22
  86.4 5.9 %convolution_subtract_fusion.2 = f32[1024,8]{0,1:T(8,128)S(1)} fusion(f32[1024,8]{0,1:T(8,128)S(1)} %get-tuple-element.123, f32[1024,1024]{1,0:T(8,128)} %get-tuple-element.122, f32[1024,8]{0,1:T(8,128)S(1)} %get-tuple-element.113), kind=kOutput, calls=%fused_computation.18.clone.1 | convolution fusion | flops 100671488 | bytes 4292608 | tf_op jit(solution)/shard_map/while/body/dot_general | solution.py:22
  92.3 3.6 %fusion.55 = f32[1024,8]{0,1:T(8,128)S(1)} fusion(f32[1024,8]{0,1:T(8,128)S(1)} %get-tuple-element.113, f32[1024,8]{0,1:T(8,128)S(1)} %convolution_subtract_fusion.2, f32[1024,1024]{1,0:T(8,128)S(1)} %copy-done), kind=kOutput, calls=%fused_computation.17.clone.1 | convolution fusion | flops 100671488 | bytes 4292608 | tf_op jit(solution)/shard_map/while/body/dot_general | solution.py:22
  96.8 37.1 %all-gather.1 = f32[32,48,8]{1,2,0:T(8,128)S(1)} all-gather(f32[1,48,8]{1,2,0:T(8,128)S(1)} %copy.98), channel_id=1, replica_groups=mesh['row'=4,'col'=8] {'row','col'}, dimensions={0}, use_global_device_ids=true | all-gather | bytes 50688 | tf_op jit(solution)/shard_map/all_gather | solution.py:82
  134.7 38.6 %all-gather.2 = f32[32,48,8]{1,2,0:T(8,128)S(1)} all-gather(f32[1,48,8]{1,2,0:T(8,128)S(1)} %convolution_bitcast_fusion.3), channel_id=1, replica_groups=mesh['row'=4,'col'=8] {'row','col'}, dimensions={0}, use_global_device_ids=true | all-gather | bytes 50688 | tf_op jit(solution)/shard_map/all_gather | solution.py:83
  173.5 1.1 scatter_custom_fusion.2
  174.9 1.3 collective-permute-start.6
  176.1 2.2 collective-permute-start.4
  178.5 1.2 scatter_custom_fusion.4
  179.8 1.3 collective-permute-start.7
  181.2 1.2 scatter_custom_fusion.3
  182.5 1.5 collective-permute-start.5
  184.1 0.7 gather_fusion.5
  185.1 0.7 gather_fusion.4
  185.9 3.0 %collective-permute-done.7 = f32[256,8]{0,1:T(8,128)S(1)} collective-permute-done((f32[256,8]{0,1:T(8,128)S(1)}, f32[256,8]{0,1:T(8,128)S(1)}, u32[]{:S(2)}, u32[]{:S(2)}) %collective-permute-start.7) | collective-permute-done | bytes 8224 | tf_op jit(solution)/shard_map/ppermute | solution.py:18
  188.9 5.6 %convolution_bitcast_fusion.1 = f32[1024,8]{0,1:T(8,128)S(1)} fusion(f32[1024,8]{0,1:T(8,128)S(1)} %maximum_add_fusion.2, f32[1,1,1024,1024]{3,2,1,0:T(8,128)} %bitcast.95), kind=kOutput, calls=%fused_computation.19 | convolution fusion | flops 100663296 | bytes 4259840 | tf_op jit(solution)/shard_map/dot_general | solution.py:22
  194.6 5.9 %collective-permute-start.10 = (f32[256,8]{0,1:T(8,128)S(1)}, f32[256,8]{0,1:T(8,128)S(1)}, u32[]{:S(2)}, u32[]{:S(2)}) collective-permute-start(f32[256,8]{0,1:T(8,128)S(1)} %get-tuple-element.53), channel_id=1, source_target_pairs={{0,8},{8,16},{16,24},{1,9},{9,17},{17,25},{2,10},{10,18},{18,26},{... | collective-permute-start | bytes 24584 | tf_op jit(solution)/shard_map/ppermute | solution.py:18
  200.6 4.0 %collective-permute-start.8 = (f32[256,8]{0,1:T(8,128)S(1)}, f32[256,8]{0,1:T(8,128)S(1)}, u32[]{:S(2)}, u32[]{:S(2)}) collective-permute-start(f32[256,8]{0,1:T(8,128)S(1)} %get-tuple-element.51), channel_id=1, source_target_pairs={{0,1},{1,2},{2,3},{3,4},{4,5},{5,6},{6,7},{8,9},{9,10},{10,11},{11... | collective-permute-start | bytes 24584 | tf_op jit(solution)/shard_map/ppermute | solution.py:18
  204.7 1.2 scatter_custom_fusion.6
  206.0 1.3 collective-permute-start.11
  207.4 1.2 scatter_custom_fusion.5
  208.7 1.3 collective-permute-start.9
  210.1 0.7 gather_fusion.7
  211.0 0.7 gather_fusion.6
  212.5 10.7 %psum.21 = f32[8]{0:T(128)S(1)} all-reduce(f32[8]{0:T(128)S(1)} %get-tuple-element.38), channel_id=1, replica_groups=mesh['row'=4,'col'=8] {'row'}, use_global_device_ids=true, to_apply=%region_8.10 | all-reduce | flops 8 | bytes 64 | tf_op jit(solution)/shard_map/psum | solution.py:11
  223.2 41.7 %psum.23 = f32[8]{0:T(128)S(1)} all-reduce(f32[8]{0:T(128)S(1)} %get-tuple-element.37), channel_id=1, replica_groups=mesh['row'=4,'col'=8] {'row','col'}, use_global_device_ids=true, to_apply=%region_13.15 | all-reduce | flops 8 | bytes 64 | tf_op jit(solution)/shard_map/psum | solution.py:93
  264.9 13.7 %psum.22 = f32[8]{0:T(128)S(1)} all-reduce(f32[8]{0:T(128)S(1)} %psum.21), channel_id=1, replica_groups=mesh['row'=4,'col'=8] {'col'}, use_global_device_ids=true, to_apply=%region_9.11 | all-reduce | flops 8 | bytes 64 | tf_op jit(solution)/shard_map/psum | solution.py:12
  278.7 0.7 subtract_bitcast_fusion
  (78 shorter events, 9.3 us)
Async XLA Ops:
  0.6 70.3 %copy-start.1 = (f32[1,1,1024,8]{2,3,1,0:T(8,128)S(1)}, f32[1,1,1024,8]{2,3,1,0:T(8,128)}, u32[]{:S(2)}) copy-start(f32[1,1,1024,8]{2,3,1,0:T(8,128)} %param.13) | copy-start | bytes 98308
  3.5 67.4 %collective-permute-start.1 = (f32[256,8]{0,1:T(8,128)S(1)}, f32[256,8]{0,1:T(8,128)S(1)}, u32[]{:S(2)}, u32[]{:S(2)}) collective-permute-start(f32[256,8]{0,1:T(8,128)S(1)} %copy.91), channel_id=1, source_target_pairs={{1,0},{2,1},{3,2},{4,3},{5,4},{6,5},{7,6},{9,8},{10,9},{11,10},{12... | collective-permute-start | bytes 24584 | tf_op jit(solution)/shard_map/ppermute | solution.py:18
  6.8 64.0 %collective-permute-start.3 = (f32[256,8]{0,1:T(8,128)S(1)}, f32[256,8]{0,1:T(8,128)S(1)}, u32[]{:S(2)}, u32[]{:S(2)}) collective-permute-start(f32[256,8]{0,1:T(8,128)S(1)} %copy.95), channel_id=1, source_target_pairs={{8,0},{16,8},{24,16},{9,1},{17,9},{25,17},{10,2},{18,10},{26,18},{... | collective-permute-start | bytes 24584 | tf_op jit(solution)/shard_map/ppermute | solution.py:18
  8.3 61.0 %collective-permute-start.2 = (f32[256,8]{1,0:T(8,128)S(1)}, f32[256,8]{1,0:T(8,128)S(1)}, u32[]{:S(2)}, u32[]{:S(2)}) collective-permute-start(f32[256,8]{1,0:T(8,128)S(1)} %bitcast.105), channel_id=1, source_target_pairs={{0,8},{8,16},{16,24},{1,9},{9,17},{17,25},{2,10},{10,18},{18,26},{... | collective-permute-start | bytes 24584 | tf_op jit(solution)/shard_map/ppermute | solution.py:18
  13.9 56.1 %collective-permute-start = (f32[256,8]{1,0:T(8,128)S(1)}, f32[256,8]{1,0:T(8,128)S(1)}, u32[]{:S(2)}, u32[]{:S(2)}) collective-permute-start(f32[256,8]{1,0:T(8,128)S(1)} %bitcast.104), channel_id=1, source_target_pairs={{0,1},{1,2},{2,3},{3,4},{4,5},{5,6},{6,7},{8,9},{9,10},{10,11},{11... | collective-permute-start | bytes 24584 | tf_op jit(solution)/shard_map/ppermute | solution.py:18
  76.9 5.9 %copy-start = (f32[1024,1024]{1,0:T(8,128)S(1)}, f32[1024,1024]{1,0:T(8,128)}, u32[]{:S(2)}) copy-start(f32[1024,1024]{1,0:T(8,128)} %get-tuple-element.124) | copy-start | bytes 12582916 | tf_op jit(solution)/shard_map/while
  86.4 5.9 %copy-start = (f32[1024,1024]{1,0:T(8,128)S(1)}, f32[1024,1024]{1,0:T(8,128)}, u32[]{:S(2)}) copy-start(f32[1024,1024]{1,0:T(8,128)} %get-tuple-element.124) | copy-start | bytes 12582916 | tf_op jit(solution)/shard_map/while
  174.9 9.1 %collective-permute-start.6 = (f32[256,8]{0,1:T(8,128)S(1)}, f32[256,8]{0,1:T(8,128)S(1)}, u32[]{:S(2)}, u32[]{:S(2)}) collective-permute-start(f32[256,8]{0,1:T(8,128)S(1)} %get-tuple-element.57), channel_id=1, source_target_pairs={{0,8},{8,16},{16,24},{1,9},{9,17},{17,25},{2,10},{10,18},{18,26},{... | collective-permute-start | bytes 24584 | tf_op jit(solution)/shard_map/ppermute | solution.py:18
  176.1 8.8 %collective-permute-start.4 = (f32[256,8]{0,1:T(8,128)S(1)}, f32[256,8]{0,1:T(8,128)S(1)}, u32[]{:S(2)}, u32[]{:S(2)}) collective-permute-start(f32[256,8]{0,1:T(8,128)S(1)} %get-tuple-element.55), channel_id=1, source_target_pairs={{0,1},{1,2},{2,3},{3,4},{4,5},{5,6},{6,7},{8,9},{9,10},{10,11},{11... | collective-permute-start | bytes 24584 | tf_op jit(solution)/shard_map/ppermute | solution.py:18
  179.8 9.1 %collective-permute-start.7 = (f32[256,8]{0,1:T(8,128)S(1)}, f32[256,8]{0,1:T(8,128)S(1)}, u32[]{:S(2)}, u32[]{:S(2)}) collective-permute-start(f32[256,8]{0,1:T(8,128)S(1)} %copy.111), channel_id=1, source_target_pairs={{8,0},{16,8},{24,16},{9,1},{17,9},{25,17},{10,2},{18,10},{26,18},{... | collective-permute-start | bytes 24584 | tf_op jit(solution)/shard_map/ppermute | solution.py:18
  182.5 6.4 %collective-permute-start.5 = (f32[256,8]{0,1:T(8,128)S(1)}, f32[256,8]{0,1:T(8,128)S(1)}, u32[]{:S(2)}, u32[]{:S(2)}) collective-permute-start(f32[256,8]{0,1:T(8,128)S(1)} %copy.107), channel_id=1, source_target_pairs={{1,0},{2,1},{3,2},{4,3},{5,4},{6,5},{7,6},{9,8},{10,9},{11,10},{12... | collective-permute-start | bytes 24584 | tf_op jit(solution)/shard_map/ppermute | solution.py:18
  194.6 15.4 %collective-permute-start.10 = (f32[256,8]{0,1:T(8,128)S(1)}, f32[256,8]{0,1:T(8,128)S(1)}, u32[]{:S(2)}, u32[]{:S(2)}) collective-permute-start(f32[256,8]{0,1:T(8,128)S(1)} %get-tuple-element.53), channel_id=1, source_target_pairs={{0,8},{8,16},{16,24},{1,9},{9,17},{17,25},{2,10},{10,18},{18,26},{... | collective-permute-start | bytes 24584 | tf_op jit(solution)/shard_map/ppermute | solution.py:18
  200.6 10.4 %collective-permute-start.8 = (f32[256,8]{0,1:T(8,128)S(1)}, f32[256,8]{0,1:T(8,128)S(1)}, u32[]{:S(2)}, u32[]{:S(2)}) collective-permute-start(f32[256,8]{0,1:T(8,128)S(1)} %get-tuple-element.51), channel_id=1, source_target_pairs={{0,1},{1,2},{2,3},{3,4},{4,5},{5,6},{6,7},{8,9},{9,10},{10,11},{11... | collective-permute-start | bytes 24584 | tf_op jit(solution)/shard_map/ppermute | solution.py:18
  206.0 6.2 %collective-permute-start.11 = (f32[256,8]{0,1:T(8,128)S(1)}, f32[256,8]{0,1:T(8,128)S(1)}, u32[]{:S(2)}, u32[]{:S(2)}) collective-permute-start(f32[256,8]{0,1:T(8,128)S(1)} %copy.119), channel_id=1, source_target_pairs={{8,0},{16,8},{24,16},{9,1},{17,9},{25,17},{10,2},{18,10},{26,18},{... | collective-permute-start | bytes 24584 | tf_op jit(solution)/shard_map/ppermute | solution.py:18
  208.7 3.7 %collective-permute-start.9 = (f32[256,8]{0,1:T(8,128)S(1)}, f32[256,8]{0,1:T(8,128)S(1)}, u32[]{:S(2)}, u32[]{:S(2)}) collective-permute-start(f32[256,8]{0,1:T(8,128)S(1)} %copy.115), channel_id=1, source_target_pairs={{1,0},{2,1},{3,2},{4,3},{5,4},{6,5},{7,6},{9,8},{10,9},{11,10},{12... | collective-permute-start | bytes 24584 | tf_op jit(solution)/shard_map/ppermute | solution.py:18
